TPU v7x, 32 devices: a whole 2x2x4 slice. The times are simulated.
32 devices in a mesh: lat: 4 (over y, x), lon: 8 (over z, core).
Axes of the slice: x: 2, y: 2, z: 4, core: 2. Of those that a mesh axis runs over, the one named last changes fastest.
Arguments:
- tracer: float32 [1152, 512, 128], P('lon', 'lat'), may hold values from -6 to 6
- courant: float32 [2, 1152, 512, 128], P(None, 'lon', 'lat'), may hold values from -0.45 to 0.45
- polar_mask: int32 [512], replicated, may hold values from 0 to 1, as said below
- cutoff: int32 [512], replicated, may hold values from 2 to 576
Outputs:
- advected: float32 [1152, 512, 128], P('lon', 'lat')
Inputs may be any that keep to these rules, and one draw needn't show every extreme that they name: polar_mask is 1 on the first a rows and on the last b rows, with a and b each between 64 and 256, and 0 on all other rows.
All inputs are finite; a program needn't handle non-finite values.
Results may differ from a plain program's by a relative error of at most 0.00007.
Values sent between devices are 32-bit elements; how exact they have to be, the bound alone decides.
A program may use at most 256 MiB of HBM per device.

v0:
```python
import math

import jax
import jax.numpy as jnp
from jax import lax
from jax.sharding import PartitionSpec as P


def extended(shard, sides, width, wrap):
    for axis, dim in sides:
        devices, length = (lax.axis_size(axis), shard.shape[dim])
        up = [(i, (i + 1) % devices) for i in range(devices if wrap else devices - 1)]
        down = [(j, i) for i, j in up]
        last = lax.slice_in_dim(shard, length - width, length, axis=dim)
        leading = lax.slice_in_dim(shard, 0, width, axis=dim)
        before = lax.ppermute(last, axis, up)
        after = lax.ppermute(leading, axis, down)
        shard = jnp.concatenate([before, shard, after], axis=dim)
    return shard


def flux_change(padded_field, padded_speed, axis, count):

    def part(array, first):
        return lax.slice_in_dim(array, first, first + count + 1, axis=axis)

    far_low = part(padded_field, 0)
    low = part(padded_field, 1)
    high = part(padded_field, 2)
    far_high = part(padded_field, 3)
    speed = part(padded_speed, 2)
    face = 7.0 / 12.0 * (low + high) - 1.0 / 12.0 * (far_low + far_high)
    limited = jnp.clip(face, jnp.minimum(low, high), jnp.maximum(low, high))
    flux = speed * limited
    return lax.slice_in_dim(flux, 1, count + 1, axis=axis) - lax.slice_in_dim(
        flux, 0, count, axis=axis
    )


def fourier_filter(circles, mask_rows, cut_rows, cos_table, sin_table):
    nlon, rows, depth = circles.shape
    half = cos_table.shape[1]
    flat = circles.reshape(nlon, rows * depth)
    highest = lax.Precision.HIGHEST
    cos_part = jnp.einsum("kw,kb->wb", cos_table, flat, precision=highest)
    sin_part = jnp.einsum("kw,kb->wb", sin_table, flat, precision=highest)
    waves = lax.broadcasted_iota(jnp.int32, (half, 1), 0)
    scale_wave = jnp.where(waves == 0, 1.0, 2.0).astype(jnp.float32) / nlon
    gains = (waves < cut_rows[None, :]).astype(jnp.float32) * scale_wave
    gains = jnp.broadcast_to(gains[:, :, None], (half, rows, depth)).reshape(half, rows * depth)
    smooth = jnp.dot(cos_table, gains * cos_part, precision=highest)
    smooth = smooth + jnp.dot(sin_table, gains * sin_part, precision=highest)
    smooth = smooth.reshape(nlon, rows, depth)
    weight = mask_rows.astype(jnp.float32)[None, :, None]
    return circles + weight * (smooth - circles)


def on_device(tracer, courant, polar_mask, cutoff):
    clon, clat, nf = tracer.shape
    lon_count = lax.axis_size("lon")
    nlon = clon * lon_count
    half = nlon // 2
    lat_index = lax.axis_index("lat")
    positions = lax.broadcasted_iota(jnp.int32, (nlon, half), 0)
    waves = lax.broadcasted_iota(jnp.int32, (nlon, half), 1)
    phase = (positions * waves % nlon).astype(jnp.float32) * (2.0 * math.pi / nlon)
    cos_table = jnp.cos(phase)
    sin_table = jnp.sin(phase)
    circles = lax.all_to_all(tracer, "lon", split_axis=2, concat_axis=0, tiled=True)
    start = lat_index * clat
    mask_rows = lax.dynamic_slice_in_dim(polar_mask, start, clat)
    cut_rows = lax.dynamic_slice_in_dim(cutoff, start, clat)
    done = fourier_filter(circles, mask_rows, cut_rows, cos_table, sin_table)
    filtered = lax.all_to_all(done, "lon", split_axis=0, concat_axis=2, tiled=True)
    lon_pair = jnp.stack([filtered, courant[0]])
    wide = extended(lon_pair, (("lon", 1),), 2, True)
    change_x = flux_change(wide[0], wide[1], 0, clon)
    lat_pair = jnp.stack([filtered, courant[1]])
    tall = extended(lat_pair, (("lat", 2),), 2, False)
    change_y = flux_change(tall[0], tall[1], 1, clat)
    return filtered - change_x - change_y


def solution(mesh):
    return jax.shard_map(
        on_device,
        mesh=mesh,
        in_specs=(P("lon", "lat", None), P(None, "lon", "lat", None), P(), P()),
        out_specs=P("lon", "lat", None),
        check_vma=False,
    )
```

profile of v0, /device:TPU:9, one launch (start us, length us, event | category | flops | bytes accessed | tf_op | source)
XLA Modules:
  0.0 948.3 jit_solution(12261988072614198197)
XLA Ops:
  25.2 192.8 %all-to-all-done = f32[144,128,128]{1,0,2:T(8,128)} async-done(((f32[144,128,128]{1,0,2:T(8,128)}), f32[144,128,128]{1,0,2:T(8,128)}, u32[]{:S(2)}, u32[]{:S(2)}) %all-to-all-start) | async-done | bytes 9437216 | tf_op jit(solution)/shard_map/all_to_all | solution.py:69
  218.0 10.2 %copy.28 = f32[8,144,128,16]{2,3,1,0:T(8,128)} copy(f32[8,144,128,16]{2,1,3,0:T(8,128)} %bitcast.2) | data formatting | bytes 18874368 | tf_op jit(solution)/shard_map/all_to_all | solution.py:69
  228.3 17.5 %copy.29 = f32[8,144,128,16]{1,0,3,2:T(8,128)} copy(f32[8,144,128,16]{2,1,3,0:T(8,128)} %bitcast.2) | data formatting | bytes 18874368 | tf_op jit(solution)/shard_map/all_to_all | solution.py:69
  245.7 16.2 %reshape.70 = f32[1152,2048]{0,1:T(8,128)} reshape(f32[8,144,128,16]{1,0,3,2:T(8,128)} %copy.29) | data formatting | bytes 18874368 | tf_op jit(solution)/shard_map/reshape | solution.py:43
  261.9 64.6 %fusion.26 = f32[576,2048]{1,0:T(8,128)} fusion(f32[1152,2048]{0,1:T(8,128)} %reshape.70), kind=kOutput, calls=%fused_computation.45 | convolution fusion | flops 16313425920 | bytes 14155776 | tf_op jit(solution)/shard_map/kw,kb->wb/dot_general | solution.py:45
  326.5 62.6 %fusion.29 = f32[576,2048]{1,0:T(8,128)S(1)} fusion(f32[1152,2048]{0,1:T(8,128)S(1)} %copy-done.2), kind=kOutput, calls=%fused_computation.46 | convolution fusion | flops 16313425920 | bytes 14155776 | tf_op jit(solution)/shard_map/kw,kb->wb/dot_general | solution.py:46
  389.1 36.7 %fusion.17 = f32[1152,2048]{1,0:T(8,128)S(1)} fusion(f32[576,2048]{1,0:T(8,128)S(1)} %bitcast.48, f32[576,2048]{1,0:T(8,128)} %fusion.26), kind=kOutput, calls=%fused_computation.35 | convolution fusion | flops 16314605568 | bytes 18874368 | tf_op jit(solution)/shard_map/dot_general | solution.py:51
  425.8 36.7 %convolution_add_fusion = f32[1152,2048]{1,0:T(8,128)} fusion(f32[1152,2048]{1,0:T(8,128)S(1)} %fusion.17, f32[576,2048]{1,0:T(8,128)S(1)} %bitcast.48, f32[576,2048]{1,0:T(8,128)S(1)} %fusion.29), kind=kOutput, calls=%fused_computation.33 | convolution fusion | flops 16316964864 | bytes 28311552 | tf_op jit(solution)/shard_map/dot_general | solution.py:52
  462.4 9.7 %copy.32 = f32[1152,2048]{0,1:T(8,128)} copy(f32[1152,2048]{1,0:T(8,128)} %convolution_add_fusion) | data formatting | bytes 18874368 | tf_op jit(solution)/shard_map/add | solution.py:52
  472.1 9.7 %copy.33 = f32[1152,128,16]{1,2,0:T(8,128)} copy(f32[1152,128,16]{0,2,1:T(8,128)} %bitcast.45) | data formatting | bytes 18874368 | tf_op jit(solution)/shard_map/reshape | solution.py:53
  481.8 10.9 %bitcast_add_fusion = f32[1152,128,16]{1,2,0:T(8,128)} fusion(f32[8,144,128,16]{2,3,1,0:T(8,128)} %copy.28, f32[1152,128,16]{1,2,0:T(8,128)} %copy.33, f32[128]{0:T(128)S(1)} %dynamic-slice_convert_fusion), kind=kLoop, calls=%fused_computation.30 | loop fusion | flops 7077888 | bytes 28312064 | tf_op jit(solution)/shard_map/add | solution.py:55
  501.3 12.1 %fusion.58 = (f32[1,144,128,128]{3,2,1,0:T(8,128)}, f32[1,144,128,128]{3,2,1,0:T(8,128)}) fusion(f32[2,144,128,128]{3,2,1,0:T(8,128)} %param.5), kind=kLoop, calls=%fused_computation.75 | loop fusion | bytes 37748736 | tf_op jit(solution)/shard_map/slice | solution.py:75
  523.0 9.7 %copy.45 = f32[1,144,128,128]{2,3,1,0:T(8,128)} copy(f32[1,144,128,128]{3,2,1,0:T(8,128)} %get-tuple-element.9) | data formatting | bytes 18874368
  532.7 171.4 %all-to-all-done.1 = f32[1152,128,16]{1,2,0:T(8,128)} async-done(((f32[1152,128,16]{1,2,0:T(8,128)}), f32[1152,128,16]{1,2,0:T(8,128)}, u32[]{:S(2)}, u32[]{:S(2)}) %all-to-all-start.1) | async-done | bytes 9437216 | tf_op jit(solution)/shard_map/all_to_all | solution.py:74
  713.1 22.2 %fusion = (f32[2,144,2,128]{2,3,1,0:T(8,128)}, f32[2,144,2,128]{2,3,1,0:T(8,128)}) fusion(f32[1,144,128,128]{2,3,1,0:T(8,128)S(1)} %bitcast.37, f32[1,144,128,128]{2,3,1,0:T(8,128)} %copy.46), kind=kLoop, calls=%fused_computation.4 | loop fusion | flops 147456 | bytes 19464192 | tf_op jit(solution)/shard_map/stack | solution.py:78
  735.3 10.9 %copy.39 = f32[2,144,2,128]{3,1,2,0:T(8,128)S(1)} copy(f32[2,144,2,128]{2,3,1,0:T(8,128)} %get-tuple-element.12) | data formatting | bytes 589824 | tf_op jit(solution)/shard_map/slice | solution.py:15
  747.5 10.9 %copy.38 = f32[2,144,2,128]{3,1,2,0:T(8,128)S(1)} copy(f32[2,144,2,128]{2,3,1,0:T(8,128)} %get-tuple-element.11) | data formatting | bytes 589824 | tf_op jit(solution)/shard_map/slice | solution.py:14
  764.9 16.2 %pad_maximum_fusion.1 = f32[2,146,128,128]{2,3,1,0:T(8,128)} fusion(f32[2,2,128,128]{2,3,1,0:T(8,128)S(1)} %collective-permute-done, f32[1,144,128,128]{2,3,1,0:T(8,128)} %copy.45, f32[1,144,128,128]{2,3,1,0:T(8,128)} %bitcast.38), kind=kLoop, calls=%fused_computation.3 | loop fusion | flops 9568256 | bytes 38273024 | tf_op jit(solution)/shard_map/concatenate | solution.py:18
  781.1 14.7 %fusion.10 = f32[1,145,128,128]{2,3,1,0:T(8,128)} fusion(f32[2,146,128,128]{2,3,1,0:T(8,128)} %pad_maximum_fusion.1, f32[2,2,128,128]{2,3,1,0:T(8,128)S(1)} %collective-permute-done.1, f32[1,144,128,128]{2,3,1,0:T(8,128)} %copy.45, f32[1,144,128,128]{2,3,1,0:T(8,128)S(1)} %bitcast.42), kind=kLoop, calls=%fused_computation.20 | loop fusion | flops 33259520 | bytes 57147392 | tf_op jit(solution)/shard_map/mul | solution.py:34
  805.3 9.8 %copy.40 = f32[2,144,2,128]{2,3,1,0:T(8,128)} copy(f32[2,144,2,128]{3,1,2,0:T(8,128)S(1)} %collective-permute-done.2) | data formatting | bytes 589824 | tf_op jit(solution)/shard_map/ppermute | solution.py:16
  815.1 31.6 %pad_maximum_fusion = f32[2,144,132,128]{2,3,1,0:T(8,128)} fusion(f32[2,144,2,128]{2,3,1,0:T(8,128)} %copy.41, f32[1,144,128,128]{2,3,1,0:T(8,128)} %copy.46, f32[1,144,128,128]{2,3,1,0:T(8,128)} %bitcast.39, f32[2,144,2,128]{2,3,1,0:T(8,128)} %copy.40), kind=kLoop, calls=%fused_computation | loop fusion | flops 14598144 | bytes 38928384 | tf_op jit(solution)/shard_map/concatenate | solution.py:18
  846.7 27.8 %slice_bitcast_fusion.1 = (f32[144,132,128]{1,2,0:T(8,128)}, f32[144,132,128]{1,2,0:T(8,128)}) fusion(f32[2,144,132,128]{2,3,1,0:T(8,128)} %pad_maximum_fusion), kind=kLoop, calls=%fused_computation.12 | loop fusion | bytes 38928384 | tf_op jit(solution)/shard_map/squeeze | solution.py:80
  874.5 43.6 %fusion.5 = f32[144,129,128]{1,2,0:T(8,128)} fusion(f32[144,132,128]{1,2,0:T(8,128)} %get-tuple-element.6, f32[144,132,128]{1,2,0:T(8,128)} %get-tuple-element.5), kind=kLoop, calls=%fused_computation.10 | loop fusion | flops 23777280 | bytes 57065472 | tf_op jit(solution)/shard_map/mul | solution.py:34
  918.1 20.5 %fusion.12 = f32[144,128,128]{1,2,0:T(8,128)} fusion(f32[144,129,128]{1,2,0:T(8,128)} %fusion.5, f32[1,145,128,128]{2,3,1,0:T(8,128)} %fusion.10, f32[144,128,8,16]{1,3,2,0:T(8,128)S(1)} %bitcast.44), kind=kLoop, calls=%fused_computation.26 | loop fusion | flops 9437184 | bytes 56623104 | tf_op jit(solution)/shard_map/sub | solution.py:81
  (47 shorter events, 79.3 us)
Async XLA Ops:
  9.6 208.4 %all-to-all-start = ((f32[144,128,128]{1,0,2:T(8,128)}), f32[144,128,128]{1,0,2:T(8,128)}, u32[]{:S(2)}, u32[]{:S(2)}) async-start(f32[144,128,128]{1,0,2:T(8,128)} %copy.26), calls=%async_computation | async-start | bytes 18874368 | tf_op jit(solution)/shard_map/all_to_all | solution.py:69
  261.9 64.6 %copy-start.2 = (f32[1152,2048]{0,1:T(8,128)S(1)}, f32[1152,2048]{0,1:T(8,128)}, u32[]{:S(2)}) copy-start(f32[1152,2048]{0,1:T(8,128)} %reshape.70) | copy-start | bytes 28311556
  261.9 127.2 %slice-start.6 = ((s8[4718592]{0:T(1024)(128)(4,1)}), s8[4194304]{0:T(1024)(128)(4,1)S(1)}, s32[]{:S(2)}) async-start(s8[4718592]{0:T(1024)(128)(4,1)} %bitcast.47), calls=%async_computation.8 | async-start | bytes 8388608
  326.4 62.6 %slice-start.7 = ((s8[4718592]{0:T(1024)(128)(4,1)}), s8[524288]{0:T(1024)(128)(4,1)S(1)}, s32[]{:S(2)}) async-start(s8[4718592]{0:T(1024)(128)(4,1)} %bitcast.47), calls=%async_computation.9 | async-start | bytes 1048576
  492.7 211.4 %all-to-all-start.1 = ((f32[1152,128,16]{1,2,0:T(8,128)}), f32[1152,128,16]{1,2,0:T(8,128)}, u32[]{:S(2)}, u32[]{:S(2)}) async-start(f32[1152,128,16]{1,2,0:T(8,128)} %bitcast_add_fusion), calls=%async_computation.1 | async-start | bytes 18874368 | tf_op jit(solution)/shard_map/all_to_all | solution.py:74
  704.1 6.5 copy-start.1
  709.4 3.8 copy-start
  710.7 54.2 %collective-permute-start = (f32[2,2,128,128]{2,3,1,0:T(8,128)S(1)}, f32[2,2,128,128]{2,3,1,0:T(8,128)S(1)}, u32[]{:S(2)}, u32[]{:S(2)}) collective-permute-start(f32[2,2,128,128]{2,3,1,0:T(8,128)S(1)} %get-tuple-element.8), channel_id=1, source_target_pairs={{1,0},{2,1},{3,2},{4,3},{5,4},{6,5},{7,6},{0,7},{9,8},{10,9},{11,1... | collective-permute-start | bytes 786440 | tf_op jit(solution)/shard_map/ppermute | solution.py:17
  746.2 49.5 %collective-permute-start.3 = (f32[2,144,2,128]{3,1,2,0:T(8,128)S(1)}, f32[2,144,2,128]{3,1,2,0:T(8,128)S(1)}, u32[]{:S(2)}, u32[]{:S(2)}) collective-permute-start(f32[2,144,2,128]{3,1,2,0:T(8,128)S(1)} %copy.39), channel_id=1, source_target_pairs={{8,0},{16,8},{24,16},{9,1},{17,9},{25,17},{10,2},{18,10},{26,18},{... | collective-permute-start | bytes 884744 | tf_op jit(solution)/shard_map/ppermute | solution.py:17
  758.5 46.8 %collective-permute-start.2 = (f32[2,144,2,128]{3,1,2,0:T(8,128)S(1)}, f32[2,144,2,128]{3,1,2,0:T(8,128)S(1)}, u32[]{:S(2)}, u32[]{:S(2)}) collective-permute-start(f32[2,144,2,128]{3,1,2,0:T(8,128)S(1)} %copy.38), channel_id=1, source_target_pairs={{0,8},{8,16},{16,24},{1,9},{9,17},{17,25},{2,10},{10,18},{18,26},{... | collective-permute-start | bytes 884744 | tf_op jit(solution)/shard_map/ppermute | solution.py:16
  762.5 18.6 %slice-start = ((s8[9437184]{0:T(1024)(128)(4,1)}), s8[4194304]{0:T(1024)(128)(4,1)S(1)}, s32[]{:S(2)}) async-start(s8[9437184]{0:T(1024)(128)(4,1)} %bitcast.40), calls=%async_computation.2 | async-start | bytes 8388608
  762.5 18.6 %slice-start.1 = ((s8[9437184]{0:T(1024)(128)(4,1)}), s8[4194304]{0:T(1024)(128)(4,1)S(1)}, s32[]{:S(2)}) async-start(s8[9437184]{0:T(1024)(128)(4,1)} %bitcast.40), calls=%async_computation.3 | async-start | bytes 8388608
  762.5 18.6 %slice-start.2 = ((s8[9437184]{0:T(1024)(128)(4,1)}), s8[1048576]{0:T(1024)(128)(4,1)S(1)}, s32[]{:S(2)}) async-start(s8[9437184]{0:T(1024)(128)(4,1)} %bitcast.40), calls=%async_computation.4 | async-start | bytes 2097152
  762.5 18.5 %collective-permute-start.1 = (f32[2,2,128,128]{2,3,1,0:T(8,128)S(1)}, f32[2,2,128,128]{2,3,1,0:T(8,128)S(1)}, u32[]{:S(2)}, u32[]{:S(2)}) collective-permute-start(f32[2,2,128,128]{2,3,1,0:T(8,128)S(1)} %get-tuple-element.7), channel_id=1, source_target_pairs={{0,1},{1,2},{2,3},{3,4},{4,5},{5,6},{6,7},{7,0},{8,9},{9,10},{10,1... | collective-permute-start | bytes 786440 | tf_op jit(solution)/shard_map/ppermute | solution.py:16
  846.7 71.4 %slice-start.3 = ((s8[9437184]{0:T(1024)(128)(4,1)}), s8[4194304]{0:T(1024)(128)(4,1)S(1)}, s32[]{:S(2)}) async-start(s8[9437184]{0:T(1024)(128)(4,1)} %bitcast.43), calls=%async_computation.5 | async-start | bytes 8388608
  846.7 71.4 %slice-start.4 = ((s8[9437184]{0:T(1024)(128)(4,1)}), s8[4194304]{0:T(1024)(128)(4,1)S(1)}, s32[]{:S(2)}) async-start(s8[9437184]{0:T(1024)(128)(4,1)} %bitcast.43), calls=%async_computation.6 | async-start | bytes 8388608
  874.5 43.6 %slice-start.5 = ((s8[9437184]{0:T(1024)(128)(4,1)}), s8[1048576]{0:T(1024)(128)(4,1)S(1)}, s32[]{:S(2)}) async-start(s8[9437184]{0:T(1024)(128)(4,1)} %bitcast.43), calls=%async_computation.7 | async-start | bytes 2097152
where the time goes:
time: 959 us; the launch traced here: 948 us
  waiting for transfers between devices  364 us (38%)
  local copies, waits for them, and re-layouts  200 us (21%)
  matrix products  200 us (21%)
  other arithmetic  160 us (17%)
  starting transfers between devices  22.4 us (2%)
    all_to_all x1, waiting for transfers between devices, on_device(): lax.all_to_all(tracer, 'lon', split_axis=2, concat_axis=0, tiled=True)  193 us
    all_to_all x1, waiting for transfers between devices, on_device(): lax.all_to_all(done, 'lon', split_axis=0, concat_axis=2, tiled=True)  171 us
    dot_general x1, matrix products, fourier_filter(): cos_part = jnp.einsum('kw,kb->wb', cos_table, flat, precision=highest)  64.6 us
    dot_general x1, matrix products, fourier_filter(): sin_part = jnp.einsum('kw,kb->wb', sin_table, flat, precision=highest)  62.6 us
    mul x2, other arithmetic, flux_change(): flux = speed * limited  58.3 us
    concatenate x2, other arithmetic, extended(): shard = jnp.concatenate([before, shard, after], axis=dim)  47.8 us
    dot_general x1, matrix products, fourier_filter(): smooth = smooth + jnp.dot(sin_table, gains * sin_part, precision=highest)  36.7 us
    dot_general x1, matrix products, fourier_filter(): smooth = jnp.dot(cos_table, gains * cos_part, precision=highest)  36.7 us
  transfers between devices with their start and end apart: 6, of which 2 were waited for; matrix products, arithmetic and copies ran while one was open for 13% of the time, Pallas kernels for 0%

commit v1 on v0

v1 whole, which is shorter than its diff:
```python
import functools
import math

import jax
import jax.numpy as jnp
import ml_dtypes
import numpy as np
from jax import lax
from jax.experimental import pallas as pl
from jax.experimental.pallas import tpu as pltpu
from jax.sharding import PartitionSpec as P

MESH = pl.DeviceIdType.MESH


def halves(table):
    high = table.astype(ml_dtypes.bfloat16)
    low = (table - high.astype(np.float64)).astype(ml_dtypes.bfloat16)
    return high, low


def hartley_tables(nlon):
    half = nlon // 2
    u = np.arange(half, dtype=np.int64)
    even = (u[:, None] * u[None, :]) % half * (2.0 * math.pi / half)
    odd = ((2 * u[:, None] + 1) * (2 * u[None, :] + 1)) % (2 * nlon) * (math.pi / nlon)
    cas = lambda t: np.cos(t) + np.sin(t)
    return (*halves(cas(even)), *halves(cas(odd)))


def split(x):
    high = x.astype(jnp.bfloat16)
    return high, (x - high.astype(jnp.float32)).astype(jnp.bfloat16)


def times(high, low, x):
    x_high, x_low = split(x)
    dot = functools.partial(jnp.dot, preferred_element_type=jnp.float32)
    return dot(high[...], x_high) + (dot(low[...], x_high) + dot(high[...], x_low))


def filter_kernel(devices, chunks, mask_ref, cut_ref, even_h, even_l, odd_h, odd_l, tracer, out,
                  ring, send_a, recv_a, self_a, send_b, recv_b, self_b):
    me = lax.axis_index("lon")
    clon, clat, nf = tracer.shape
    rows = clat // devices
    size = rows // chunks
    nlon = clon * devices
    half = nlon // 2
    first_row = lax.axis_index("lat") * clat + me * rows
    peers = [lax.rem(me + off, devices) for off in range(1, devices)]

    barrier = pltpu.get_barrier_semaphore()
    for peer in peers:
        pl.semaphore_signal(barrier, inc=1, device_id={"lon": peer}, device_id_type=MESH)
    pl.semaphore_wait(barrier, devices - 1)

    def source(owner, c):
        return tracer.at[:, pl.ds(pl.multiple_of(owner * rows + c * size, size), size), :]

    def landing(c):
        return ring.at[c, pl.ds(2 + me * clon, clon)]

    def result(owner, c):
        return ring.at[c, pl.ds(owner * clon, clon + 4)]

    def home(c):
        return out.at[:, pl.ds(pl.multiple_of(me * rows + c * size, size), size), :]

    there, back = [], []
    for c in range(chunks):
        own = pltpu.make_async_copy(source(me, c), landing(c), self_a.at[c])
        sent = [
            pltpu.make_async_remote_copy(
                source(peer, c), landing(c), send_a.at[c, j], recv_a.at[c, j],
                device_id={"lon": peer}, device_id_type=MESH)
            for j, peer in enumerate(peers)
        ]
        own.start()
        for copy in sent:
            copy.start()
        there.append((own, sent))

    lane = lax.broadcasted_iota(jnp.int32, (1, 2 * nf), 1)
    index = lax.broadcasted_iota(jnp.int32, (half, 2 * nf), 0)
    scale = 1.0 / nlon

    for c in range(chunks):
        own, sent = there[c]
        own.wait()
        for copy in sent:
            copy.wait_recv()
        flat = ring.at[c].reshape((nlon + 4) * size, nf)

        def pair(p, carry):
            def block(start, count, r):
                return (pl.ds(start * size + r, count, stride=size), slice(None))

            def load(start):
                return jnp.concatenate(
                    [flat[block(start, half, 2 * p + s)] for s in range(2)], axis=1)

            row = first_row + c * size + 2 * p
            cut = jnp.where(lane < nf, cut_ref[row], cut_ref[row + 1])
            mask = jnp.where(lane < nf, mask_ref[row], mask_ref[row + 1])
            low, high = load(2), load(2 + half)
            even = times(even_h, even_l, low + high)
            odd = times(odd_h, odd_l, low - high)
            wave = 2 * index
            even = jnp.where(jnp.minimum(wave, nlon - wave) < cut, even * scale, 0.0)
            odd = jnp.where(jnp.minimum(wave + 1, nlon - 1 - wave) < cut, odd * scale, 0.0)
            even = times(even_h, even_l, even)
            odd = times(odd_h, odd_l, odd)
            low = jnp.where(mask > 0, even + odd, low)
            high = jnp.where(mask > 0, even - odd, high)
            for s in range(2):
                r = 2 * p + s
                lo, hi = low[:, s * nf:(s + 1) * nf], high[:, s * nf:(s + 1) * nf]
                flat[block(2, half, r)] = lo
                flat[block(2 + half, half, r)] = hi
                for e in range(2):
                    flat[pl.ds((2 + nlon + e) * size + r, 1), :] = lo[e:e + 1]
                    flat[pl.ds(e * size + r, 1), :] = hi[half - 2 + e:half - 1 + e]
            return carry

        lax.fori_loop(0, size // 2, pair, 0)

        own = pltpu.make_async_copy(result(me, c), home(c), self_b.at[c])
        sent = [
            pltpu.make_async_remote_copy(
                result(peer, c), home(c), send_b.at[c, j], recv_b.at[c, j],
                device_id={"lon": peer}, device_id_type=MESH)
            for j, peer in enumerate(peers)
        ]
        own.start()
        for copy in sent:
            copy.start()
        back.append((own, sent))

    for c in range(chunks):
        for copy in there[c][1]:
            copy.wait_send()
        own, sent = back[c]
        own.wait()
        for copy in sent:
            copy.wait()


def filtered_columns(tracer, polar_mask, cutoff, devices):
    clon, clat, nf = tracer.shape
    nlon = clon * devices
    rows = clat // devices
    chunks = rows // 8
    size = rows // chunks
    tables = [jnp.asarray(t) for t in hartley_tables(nlon)]
    smem = pl.BlockSpec(memory_space=pltpu.SMEM)
    vmem = pl.BlockSpec(memory_space=pltpu.VMEM)
    hbm = pl.BlockSpec(memory_space=pl.ANY)
    pairs = pltpu.SemaphoreType.DMA((chunks, devices - 1))
    alone = pltpu.SemaphoreType.DMA((chunks,))
    return pl.pallas_call(
        functools.partial(filter_kernel, devices, chunks),
        out_shape=jax.ShapeDtypeStruct((clon + 4, clat, nf), jnp.float32),
        in_specs=[smem, smem, vmem, vmem, vmem, vmem, hbm],
        out_specs=hbm,
        scratch_shapes=[pltpu.VMEM((chunks, nlon + 4, size, nf), jnp.float32),
                        pairs, pairs, alone, pairs, pairs, alone],
        compiler_params=pltpu.CompilerParams(
            collective_id=0, has_side_effects=True, vmem_limit_bytes=48 << 20),
        name="filter_exchange",
    )(polar_mask, cutoff, *tables, tracer)


def limited(far_low, low, high, far_high):
    face = (7.0 / 12.0) * (low + high) - (1.0 / 12.0) * (far_low + far_high)
    return jnp.minimum(jnp.maximum(face, jnp.minimum(low, high)), jnp.maximum(low, high))


def flux_kernel(field, speed_x, next_x, edge_x, speed_y, edge_y, before, after, out, tall, flux):
    count, clat = out.shape[0], out.shape[1]
    final = pl.program_id(0) == pl.num_programs(0) - 1

    def flux_x(i, speed):
        return speed * limited(field[i], field[i + 1], field[i + 2], field[i + 3])

    def column(c, low_flux, speed):
        high_flux = flux_x(c + 1, speed)
        value = field[c + 2]
        tall[8:8 + clat] = value
        tall[6:8] = before[c]
        tall[8 + clat:10 + clat] = after[c]
        flux[0:clat] = speed_y[c] * limited(
            tall[6:6 + clat], tall[7:7 + clat], value, tall[9:9 + clat])
        flux[clat:clat + 1] = edge_y[c] * limited(
            tall[6 + clat:7 + clat], tall[7 + clat:8 + clat],
            tall[8 + clat:9 + clat], tall[9 + clat:10 + clat])
        out[c] = value - (high_flux - low_flux) - (flux[1:clat + 1] - flux[0:clat])
        return high_flux

    carry = flux_x(0, speed_x[0])
    carry = lax.fori_loop(0, count - 1, lambda c, low: column(c, low, speed_x[c + 1]), carry)
    column(count - 1, carry, jnp.where(final, edge_x[0], next_x[0]))


def advect(field, courant, edge_x, edge_y, before, after):
    _, clon, clat, nf = courant.shape
    block = math.gcd(clon, 16)
    squeezed = pl.Squeezed()
    return pl.pallas_call(
        flux_kernel,
        grid=(clon // block,),
        out_shape=jax.ShapeDtypeStruct((clon, clat, nf), jnp.float32),
        in_specs=[
            pl.BlockSpec((pl.Element(block + 4), pl.Element(clat), pl.Element(nf)),
                         lambda i: (i * block, 0, 0)),
            pl.BlockSpec((squeezed, block, clat, nf), lambda i: (0, i, 0, 0)),
            pl.BlockSpec((squeezed, 1, clat, nf),
                         lambda i: (0, jnp.minimum((i + 1) * block, clon - 1), 0, 0)),
            pl.BlockSpec((1, clat, nf), lambda i: (0, 0, 0)),
            pl.BlockSpec((squeezed, block, clat, nf), lambda i: (1, i, 0, 0)),
            pl.BlockSpec((block, 1, nf), lambda i: (i, 0, 0)),
            pl.BlockSpec((block, 2, nf), lambda i: (i, 0, 0)),
            pl.BlockSpec((block, 2, nf), lambda i: (i, 0, 0)),
        ],
        out_specs=pl.BlockSpec((block, clat, nf), lambda i: (i, 0, 0)),
        scratch_shapes=[pltpu.VMEM((clat + 16, nf), jnp.float32),
                        pltpu.VMEM((clat + 8, nf), jnp.float32)],
        compiler_params=pltpu.CompilerParams(vmem_limit_bytes=48 << 20),
        name="flux_step",
    )(field, courant, courant, edge_x, courant, edge_y, before, after)


def filtered_by_collectives(tracer, polar_mask, cutoff, devices):
    clon, clat, nf = tracer.shape
    nlon, half = clon * devices, clon * devices // 2
    circles = lax.all_to_all(tracer, "lon", split_axis=1, concat_axis=0, tiled=True)
    rows = clat // devices
    start = lax.axis_index("lat") * clat + lax.axis_index("lon") * rows
    mask = lax.dynamic_slice_in_dim(polar_mask, start, rows)[None, :, None]
    cut = lax.dynamic_slice_in_dim(cutoff, start, rows)[None, :, None]
    tables = [jnp.asarray(t).astype(jnp.float32) for t in hartley_tables(nlon)]
    apply = lambda h, l, x: jnp.einsum("uk,krc->urc", h + l, x, precision=lax.Precision.HIGHEST)
    low, high = circles[:half], circles[half:]
    wave = 2 * lax.broadcasted_iota(jnp.int32, (half, 1, 1), 0)
    even = apply(tables[0], tables[1], low + high) * (1.0 / nlon)
    odd = apply(tables[2], tables[3], low - high) * (1.0 / nlon)
    even = jnp.where(jnp.minimum(wave, nlon - wave) < cut, even, 0.0)
    odd = jnp.where(jnp.minimum(wave + 1, nlon - 1 - wave) < cut, odd, 0.0)
    even = apply(tables[0], tables[1], even)
    odd = apply(tables[2], tables[3], odd)
    smooth = jnp.concatenate([even + odd, even - odd], axis=0)
    done = jnp.where(mask > 0, smooth, circles)
    field = lax.all_to_all(done, "lon", split_axis=0, concat_axis=1, tiled=True)
    up = [(i, (i + 1) % devices) for i in range(devices)]
    down = [(j, i) for i, j in up]
    before = lax.ppermute(field[clon - 2:], "lon", up)
    after = lax.ppermute(field[:2], "lon", down)
    return jnp.concatenate([before, field, after], axis=0)


def on_device(tracer, courant, polar_mask, cutoff):
    clon, clat, nf = tracer.shape
    devices, bands = lax.axis_size("lon"), lax.axis_size("lat")
    west = [((i + 1) % devices, i) for i in range(devices)]
    south = [(i, i + 1) for i in range(bands - 1)]
    north = [(j, i) for i, j in south]
    edge_x = lax.ppermute(courant[0, :1], "lon", west)
    edge_y = lax.ppermute(courant[1, :, :1], "lat", north)
    whole = clat % (8 * devices) == 0
    build = filtered_columns if whole else filtered_by_collectives
    field = build(tracer, polar_mask, cutoff, devices)
    before = lax.ppermute(field[2:2 + clon, clat - 2:], "lat", south)
    after = lax.ppermute(field[2:2 + clon, :2], "lat", north)
    return advect(field, courant, edge_x, edge_y, before, after)


def solution(mesh):
    return jax.shard_map(
        on_device,
        mesh=mesh,
        in_specs=(P("lon", "lat", None), P(None, "lon", "lat", None), P(), P()),
        out_specs=P("lon", "lat", None),
        check_vma=False,
    )
```

time: 959 us -> 459 us (0.48)
  Pallas kernels: 0 us -> 435 us
  waiting for transfers between devices: 364 us -> 3.7 us
  matrix products: 200 us -> 0 us
  local copies, waits for them, and re-layouts: 200 us -> 9.13 us
  other arithmetic: 160 us -> 0 us
  starting transfers between devices: 22.4 us -> 7.49 us
    pallas_call x0 -> x2, Pallas kernels: none -> 435 us  [the longest x1 416 us: filtered_columns(): pl.pallas_call(functools.partial(filter_kernel, devices, chunks), out_sha...]
    all_to_all x2 -> x0, waiting for transfers between devices: 364 us -> none  [the longest x1 193 us: on_device(): lax.all_to_all(tracer, 'lon', split_axis=2, concat_axis=0, tiled=True)]
    dot_general x4 -> x0, matrix products: 200 us -> none  [the longest x1 64.6 us: fourier_filter(): cos_part = jnp.einsum('kw,kb->wb', cos_table, flat, precision=highest)]
    mul x3 -> x0, other arithmetic: 58.3 us -> none  [the longest x2 58.3 us: flux_change(): flux = speed * limited]
    concatenate x2 -> x0, other arithmetic: 47.8 us -> none  [extended(): shard = jnp.concatenate([before, shard, after], axis=dim)]
    all_to_all x3 -> x0, local copies, waits for them, and re-layouts: 33 us -> none  [the longest x2 27.7 us: on_device(): lax.all_to_all(tracer, 'lon', split_axis=2, concat_axis=0, tiled=True)]
    slice x3 -> x1, local copies, waits for them, and re-layouts: 33.9 us -> 1.36 us  [on_device(): after = lax.ppermute(field[2:2 + clon, :2], 'lat', north)]
    reshape x3 -> x0, local copies, waits for them, and re-layouts: 31.6 us -> none  [the longest x1 16.2 us: fourier_filter(): flat = circles.reshape(nlon, rows * depth)]
  transfers between devices with their start and end apart: 6 -> 4, of which waited for: 2 -> 1; matrix products, arithmetic and copies ran while one was open for 13% -> 0% of each run, Pallas kernels for 0% -> 91%
where the time goes in v1:
time: 459 us; the launch traced here: 456 us
  Pallas kernels  435 us (95%)
  local copies, waits for them, and re-layouts  9.13 us (2%)
  starting transfers between devices  7.49 us (2%)
    pallas_call x1, Pallas kernels, filtered_columns(): pl.pallas_call(functools.partial(filter_kernel, devices, chunks), out_sha...  416 us
    pallas_call x1, Pallas kernels, advect(): pl.pallas_call(flux_kernel, grid=(clon // block,), out_shape=jax.ShapeDty...  19.4 us
  transfers between devices with their start and end apart: 4, of which 1 were waited for; matrix products, arithmetic and copies ran while one was open for 0% of the time, Pallas kernels for 91%

profile of v1, /device:TPU:9, one launch (start us, length us, event | category | flops | bytes accessed | tf_op | source)
XLA Modules:
  0.0 455.6 jit_solution(3885990320938294758)
XLA Ops:
  0.0 1.1 slice_bitcast_fusion
  1.1 1.3 collective-permute-start.1
  2.4 0.0 copy-start
  2.4 1.1 copy-done
  3.5 0.0 copy-start.1
  3.5 1.1 copy-done.1
  4.6 0.0 copy-start.2
  4.6 1.1 copy-done.2
  5.8 0.0 copy-start.3
  5.8 1.1 copy-done.3
  6.9 0.0 copy-start.4
  6.9 0.7 copy-done.4
  7.6 0.7 copy-done.5
  8.2 415.8 %filter_exchange.1.field = f32[148,128,128]{2,1,0:T(8,128)} custom-call(s32[512]{0:T(512)S(1)} %copy-done.4, s32[512]{0:T(512)S(1)} %copy-done.5, bf16[576,576]{1,0:T(8,128)(2,1)S(1)} %copy-done.3, bf16[576,576]{1,0:T(8,128)(2,1)S(1)} %copy-done.2, bf16[576,576]{1,0:T(8,128)(2,1)S(1)} %copy-done.1, bf16[576,576]{1,0:T(8,128)(2,1)S(1)} %copy-done, ...), custom_call_target="tpu_custom_call" | custom-call | tf_op jit(solution)/shard_map/filter_exchange/pallas_call | solution.py:161
  424.1 1.4 fusion
  425.4 1.3 collective-permute-start.3
  426.7 4.9 %collective-permute-start.2 = (f32[144,2,128]{2,1,0:T(2,128)S(1)}, f32[144,2,128]{2,1,0:T(2,128)S(1)}, u32[]{:S(2)}, u32[]{:S(2)}) collective-permute-start(f32[144,2,128]{2,1,0:T(2,128)S(1)} %get-tuple-element.6), channel_id=1, source_target_pairs={{0,8},{8,16},{16,24},{1,9},{9,17},{17,25},{2,10},{10,18},{18,26},{... | collective-permute-start | bytes 442376 | tf_op jit(solution)/shard_map/ppermute | solution.py:272
  431.6 0.8 slice_bitcast_fusion.1
  432.5 0.0 collective-permute-start
  432.5 3.7 collective-permute-done.edge_x
  436.2 0.0 collective-permute-done.1.edge_y
  436.2 0.0 collective-permute-done.3.after
  436.2 0.0 collective-permute-done.2.before
  436.2 19.4 %flux_step.1 = f32[144,128,128]{2,1,0:T(8,128)} custom-call(f32[148,128,128]{2,1,0:T(8,128)} %filter_exchange.1.field, f32[2,144,128,128]{3,2,1,0:T(8,128)} %speed_y.1, f32[2,144,128,128]{3,2,1,0:T(8,128)} %speed_y.1, f32[1,128,128]{2,1,0:T(8,128)S(1)} %collective-permute-done.edge_x, f32[2,144,128,128]{3,2,1,0:T(8,128)} %speed_y.1, ...), custom_call_target="tpu_custom_call" | custom-call | tf_op jit(solution)/shard_map/flux_step/pallas_call | solution.py:209
  (1 shorter events, 0.0 us)
Async XLA Ops:
  1.1 435.1 %collective-permute-start.1 = (f32[144,1,128]{2,1,0:T(1,128)S(1)}, f32[144,1,128]{2,1,0:T(1,128)S(1)}, u32[]{:S(2)}, u32[]{:S(2)}) collective-permute-start(f32[144,1,128]{2,1,0:T(1,128)S(1)} %slice_bitcast_fusion), channel_id=1, source_target_pairs={{8,0},{16,8},{24,16},{9,1},{17,9},{25,17},{10,2},{18,10},{26,18},{... | collective-permute-start | bytes 221192 | tf_op jit(solution)/shard_map/ppermute | solution.py:268
  2.4 1.1 copy-start
  3.5 1.1 copy-start.1
  4.6 1.1 copy-start.2
  5.8 1.1 copy-start.3
  6.9 0.7 copy-start.4
  7.6 0.7 copy-start.5
  425.4 10.8 %collective-permute-start.3 = (f32[144,2,128]{2,1,0:T(2,128)S(1)}, f32[144,2,128]{2,1,0:T(2,128)S(1)}, u32[]{:S(2)}, u32[]{:S(2)}) collective-permute-start(f32[144,2,128]{2,1,0:T(2,128)S(1)} %get-tuple-element.5), channel_id=1, source_target_pairs={{8,0},{16,8},{24,16},{9,1},{17,9},{25,17},{10,2},{18,10},{26,18},{... | collective-permute-start | bytes 442376 | tf_op jit(solution)/shard_map/ppermute | solution.py:273
  426.7 9.5 %collective-permute-start.2 = (f32[144,2,128]{2,1,0:T(2,128)S(1)}, f32[144,2,128]{2,1,0:T(2,128)S(1)}, u32[]{:S(2)}, u32[]{:S(2)}) collective-permute-start(f32[144,2,128]{2,1,0:T(2,128)S(1)} %get-tuple-element.6), channel_id=1, source_target_pairs={{0,8},{8,16},{16,24},{1,9},{9,17},{17,25},{2,10},{10,18},{18,26},{... | collective-permute-start | bytes 442376 | tf_op jit(solution)/shard_map/ppermute | solution.py:272
  432.5 3.7 collective-permute-start

commit v2 on v1

--- a/solution.py
+++ b/solution.py
@@ -39,24 +39,38 @@
     return dot(high[...], x_high) + (dot(low[...], x_high) + dot(high[...], x_low))
 
 
-def filter_kernel(devices, chunks, mask_ref, cut_ref, even_h, even_l, odd_h, odd_l, tracer, out,
-                  ring, send_a, recv_a, self_a, send_b, recv_b, self_b):
-    me = lax.axis_index("lon")
+def filter_kernel(devices, bands, chunks, mask_ref, cut_ref, tracer, courant, *rest):
+    tables, rest = rest[:4], rest[4:]
+    (out, before, after, edge_x, edge_y, ring, even_h, even_l, odd_h, odd_l,
+     table_sem, send_a, recv_a, self_a, send_b, recv_b, self_b, send_e, recv_e) = rest
+    me, lat = lax.axis_index("lon"), lax.axis_index("lat")
     clon, clat, nf = tracer.shape
-    rows = clat // devices
-    size = rows // chunks
+    size = clat // devices // chunks
     nlon = clon * devices
     half = nlon // 2
-    first_row = lax.axis_index("lat") * clat + me * rows
-    peers = [lax.rem(me + off, devices) for off in range(1, devices)]
+    order = sorted(range(1, devices), key=lambda off: -min(off, devices - off))
+    peers = [lax.rem(me + off, devices) for off in order]
+    west = lax.rem(me + devices - 1, devices)
+    north, south = lax.rem(lat + bands - 1, bands), lax.rem(lat + 1, bands)
+
+    loads = [
+        pltpu.make_async_copy(table, place, table_sem.at[i])
+        for i, (table, place) in enumerate(zip(tables, (even_h, even_l, odd_h, odd_l)))
+    ]
+    for copy in loads:
+        copy.start()
 
     barrier = pltpu.get_barrier_semaphore()
     for peer in peers:
         pl.semaphore_signal(barrier, inc=1, device_id={"lon": peer}, device_id_type=MESH)
-    pl.semaphore_wait(barrier, devices - 1)
-
-    def source(owner, c):
-        return tracer.at[:, pl.ds(pl.multiple_of(owner * rows + c * size, size), size), :]
+    for band in (north, south):
+        pl.semaphore_signal(barrier, inc=1, device_id={"lat": band}, device_id_type=MESH)
+    pl.semaphore_wait(barrier, devices + 1)
+
+    def first(owner, c):
+        flip = owner // (devices // 2)
+        tile = owner * chunks + c + flip * (chunks - 1 - 2 * c)
+        return pl.multiple_of(tile * size, size)
 
     def landing(c):
         return ring.at[c, pl.ds(2 + me * clon, clon)]
@@ -65,7 +79,10 @@
         return ring.at[c, pl.ds(owner * clon, clon + 4)]
 
     def home(c):
-        return out.at[:, pl.ds(pl.multiple_of(me * rows + c * size, size), size), :]
+        return out.at[:, pl.ds(first(me, c), size), :]
+
+    def source(owner, c):
+        return tracer.at[:, pl.ds(first(owner, c), size), :]
 
     there, back = [], []
     for c in range(chunks):
@@ -77,9 +94,27 @@
             for j, peer in enumerate(peers)
         ]
         own.start()
-        for copy in sent:
+        for j, copy in enumerate(sent):
+            if c:
+                there[-1][1][j].wait_send()
             copy.start()
         there.append((own, sent))
+
+    def edge(src, dst, k, device):
+        return pltpu.make_async_remote_copy(
+            src, dst, send_e.at[k], recv_e.at[k], device_id=device, device_id_type=MESH)
+
+    def inner(ref, start):
+        return ref.at[pl.ds(2, clon), pl.ds(start, 8), :]
+
+    go_x = edge(courant.at[0, pl.ds(0, 1)], edge_x, 0, {"lon": west})
+    go_y = edge(courant.at[1, :, pl.ds(0, 8), :], edge_y, 1, {"lat": north})
+    go_north = edge(inner(out, 0), after, 2, {"lat": north})
+    go_south = edge(inner(out, clat - 8), before, 3, {"lat": south})
+    go_x.start()
+    go_y.start()
+    for copy in loads:
+        copy.wait()
 
     lane = lax.broadcasted_iota(jnp.int32, (1, 2 * nf), 1)
     index = lax.broadcasted_iota(jnp.int32, (half, 2 * nf), 0)
@@ -91,6 +126,7 @@
         for copy in sent:
             copy.wait_recv()
         flat = ring.at[c].reshape((nlon + 4) * size, nf)
+        first_row = lat * clat + first(me, c)
 
         def pair(p, carry):
             def block(start, count, r):
@@ -100,7 +136,7 @@
                 return jnp.concatenate(
                     [flat[block(start, half, 2 * p + s)] for s in range(2)], axis=1)
 
-            row = first_row + c * size + 2 * p
+            row = first_row + 2 * p
             cut = jnp.where(lane < nf, cut_ref[row], cut_ref[row + 1])
             mask = jnp.where(lane < nf, mask_ref[row], mask_ref[row + 1])
             low, high = load(2), load(2 + half)
@@ -137,38 +173,59 @@
             copy.start()
         back.append((own, sent))
 
+    for copy in there[-1][1]:
+        copy.wait_send()
+    go_x.wait()
     for c in range(chunks):
-        for copy in there[c][1]:
-            copy.wait_send()
         own, sent = back[c]
         own.wait()
         for copy in sent:
             copy.wait()
-
-
-def filtered_columns(tracer, polar_mask, cutoff, devices):
+        if c == 0:
+            @pl.when(lat > 0)
+            def _():
+                go_north.start()
+
+            @pl.when(lat < bands - 1)
+            def _():
+                go_south.start()
+    go_y.wait()
+
+    @pl.when(lat > 0)
+    def _():
+        go_north.wait_send()
+        go_south.wait_recv()
+
+    @pl.when(lat < bands - 1)
+    def _():
+        go_south.wait_send()
+        go_north.wait_recv()
+
+
+def by_kernel(tracer, courant, polar_mask, cutoff, devices, bands):
     clon, clat, nf = tracer.shape
     nlon = clon * devices
-    rows = clat // devices
-    chunks = rows // 8
-    size = rows // chunks
+    half = nlon // 2
+    chunks = clat // devices // 8
     tables = [jnp.asarray(t) for t in hartley_tables(nlon)]
     smem = pl.BlockSpec(memory_space=pltpu.SMEM)
-    vmem = pl.BlockSpec(memory_space=pltpu.VMEM)
     hbm = pl.BlockSpec(memory_space=pl.ANY)
-    pairs = pltpu.SemaphoreType.DMA((chunks, devices - 1))
-    alone = pltpu.SemaphoreType.DMA((chunks,))
+    dma = pltpu.SemaphoreType.DMA
+    pairs, alone = dma((chunks, devices - 1)), dma((chunks,))
+    shape = lambda *dims: jax.ShapeDtypeStruct(dims, jnp.float32)
+    edge = shape(clon, 8, nf)
     return pl.pallas_call(
-        functools.partial(filter_kernel, devices, chunks),
-        out_shape=jax.ShapeDtypeStruct((clon + 4, clat, nf), jnp.float32),
-        in_specs=[smem, smem, vmem, vmem, vmem, vmem, hbm],
-        out_specs=hbm,
-        scratch_shapes=[pltpu.VMEM((chunks, nlon + 4, size, nf), jnp.float32),
-                        pairs, pairs, alone, pairs, pairs, alone],
+        functools.partial(filter_kernel, devices, bands, chunks),
+        out_shape=(shape(clon + 4, clat, nf), edge, edge, shape(1, clat, nf), edge),
+        in_specs=[smem, smem] + [hbm] * 6,
+        out_specs=(hbm,) * 5,
+        scratch_shapes=[pltpu.VMEM((chunks, nlon + 4, 8, nf), jnp.float32)]
+        + [pltpu.VMEM((half, half), jnp.bfloat16)] * 4
+        + [dma((4,)), pairs, pairs, alone, pairs, pairs, alone, dma((4,)), dma((4,))],
         compiler_params=pltpu.CompilerParams(
             collective_id=0, has_side_effects=True, vmem_limit_bytes=48 << 20),
         name="filter_exchange",
-    )(polar_mask, cutoff, *tables, tracer)
+    )(polar_mask, cutoff, tracer, courant, *tables)
 
 
 def limited(far_low, low, high, far_high):
@@ -176,9 +233,11 @@
     return jnp.minimum(jnp.maximum(face, jnp.minimum(low, high)), jnp.maximum(low, high))
 
 
-def flux_kernel(field, speed_x, next_x, edge_x, speed_y, edge_y, before, after, out, tall, flux):
+def flux_kernel(bands, field, speed_x, next_x, edge_x, speed_y, edge_y, before, after, out, tall, flux):
     count, clat = out.shape[0], out.shape[1]
     final = pl.program_id(0) == pl.num_programs(0) - 1
+    lat = lax.axis_index("lat")
+    top, bottom = lat > 0, lat < bands - 1
 
     def flux_x(i, speed):
         return speed * limited(field[i], field[i + 1], field[i + 2], field[i + 3])
@@ -187,11 +246,11 @@
         high_flux = flux_x(c + 1, speed)
         value = field[c + 2]
         tall[8:8 + clat] = value
-        tall[6:8] = before[c]
-        tall[8 + clat:10 + clat] = after[c]
+        tall[0:8] = jnp.where(top, before[c], 0.0)
+        tall[8 + clat:16 + clat] = jnp.where(bottom, after[c], 0.0)
         flux[0:clat] = speed_y[c] * limited(
             tall[6:6 + clat], tall[7:7 + clat], value, tall[9:9 + clat])
-        flux[clat:clat + 1] = edge_y[c] * limited(
+        flux[clat:clat + 1] = jnp.where(bottom, edge_y[c, 0:1], 0.0) * limited(
             tall[6 + clat:7 + clat], tall[7 + clat:8 + clat],
             tall[8 + clat:9 + clat], tall[9 + clat:10 + clat])
         out[c] = value - (high_flux - low_flux) - (flux[1:clat + 1] - flux[0:clat])
@@ -202,12 +261,12 @@
     column(count - 1, carry, jnp.where(final, edge_x[0], next_x[0]))
 
 
-def advect(field, courant, edge_x, edge_y, before, after):
+def advect(field, before, after, edge_x, edge_y, courant, bands):
     _, clon, clat, nf = courant.shape
     block = math.gcd(clon, 16)
     squeezed = pl.Squeezed()
     return pl.pallas_call(
-        flux_kernel,
+        functools.partial(flux_kernel, bands),
         grid=(clon // block,),
         out_shape=jax.ShapeDtypeStruct((clon, clat, nf), jnp.float32),
         in_specs=[
@@ -218,9 +277,9 @@
                          lambda i: (0, jnp.minimum((i + 1) * block, clon - 1), 0, 0)),
             pl.BlockSpec((1, clat, nf), lambda i: (0, 0, 0)),
             pl.BlockSpec((squeezed, block, clat, nf), lambda i: (1, i, 0, 0)),
-            pl.BlockSpec((block, 1, nf), lambda i: (i, 0, 0)),
-            pl.BlockSpec((block, 2, nf), lambda i: (i, 0, 0)),
-            pl.BlockSpec((block, 2, nf), lambda i: (i, 0, 0)),
+            pl.BlockSpec((block, 8, nf), lambda i: (i, 0, 0)),
+            pl.BlockSpec((block, 8, nf), lambda i: (i, 0, 0)),
+            pl.BlockSpec((block, 8, nf), lambda i: (i, 0, 0)),
         ],
         out_specs=pl.BlockSpec((block, clat, nf), lambda i: (i, 0, 0)),
         scratch_shapes=[pltpu.VMEM((clat + 16, nf), jnp.float32),
@@ -230,7 +289,7 @@
     )(field, courant, courant, edge_x, courant, edge_y, before, after)
 
 
-def filtered_by_collectives(tracer, polar_mask, cutoff, devices):
+def by_collectives(tracer, courant, polar_mask, cutoff, devices, bands):
     clon, clat, nf = tracer.shape
     nlon, half = clon * devices, clon * devices // 2
     circles = lax.all_to_all(tracer, "lon", split_axis=1, concat_axis=0, tiled=True)
@@ -255,23 +314,22 @@
     down = [(j, i) for i, j in up]
     before = lax.ppermute(field[clon - 2:], "lon", up)
     after = lax.ppermute(field[:2], "lon", down)
-    return jnp.concatenate([before, field, after], axis=0)
-
-
-def on_device(tracer, courant, polar_mask, cutoff):
-    clon, clat, nf = tracer.shape
-    devices, bands = lax.axis_size("lon"), lax.axis_size("lat")
-    west = [((i + 1) % devices, i) for i in range(devices)]
+    wide = jnp.concatenate([before, field, after], axis=0)
     south = [(i, i + 1) for i in range(bands - 1)]
     north = [(j, i) for i, j in south]
-    edge_x = lax.ppermute(courant[0, :1], "lon", west)
-    edge_y = lax.ppermute(courant[1, :, :1], "lat", north)
-    whole = clat % (8 * devices) == 0
-    build = filtered_columns if whole else filtered_by_collectives
-    field = build(tracer, polar_mask, cutoff, devices)
-    before = lax.ppermute(field[2:2 + clon, clat - 2:], "lat", south)
-    after = lax.ppermute(field[2:2 + clon, :2], "lat", north)
-    return advect(field, courant, edge_x, edge_y, before, after)
+    edge_x = lax.ppermute(courant[0, :1], "lon", down)
+    edge_y = lax.ppermute(courant[1, :, :8], "lat", north)
+    before = lax.ppermute(field[:, clat - 8:], "lat", south)
+    after = lax.ppermute(field[:, :8], "lat", north)
+    return wide, before, after, edge_x, edge_y
+
+
+def on_device(tracer, courant, polar_mask, cutoff):
+    devices, bands = lax.axis_size("lon"), lax.axis_size("lat")
+    fits = tracer.shape[1] % (8 * devices) == 0 and bands > 2
+    build = by_kernel if fits else by_collectives
+    parts = build(tracer, courant, polar_mask, cutoff, devices, bands)
+    return advect(*parts, courant, bands)
 
 
 def solution(mesh):

time: 459 us -> 444 us (0.967)
  starting transfers between devices: 7.49 us -> 0 us
    ppermute x4 -> x0, starting transfers between devices: 7.49 us -> none  [the longest x1 4.9 us: on_device(): before = lax.ppermute(field[2:2 + clon, clat - 2:], 'lat', south)]
  transfers between devices with their start and end apart: 4 -> 0, of which waited for: 1 -> 0; matrix products, arithmetic and copies ran while one was open for 0% -> 0% of each run, Pallas kernels for 91% -> 0%
where the time goes in v2:
time: 444 us
  Pallas kernels  438 us (99%)
  local copies, waits for them, and re-layouts  5.82 us (1%)
    pallas_call x1, Pallas kernels, by_kernel(): pl.pallas_call(functools.partial(filter_kernel, devices, bands, chunks),...  418 us
    pallas_call x1, Pallas kernels, advect(): pl.pallas_call(functools.partial(flux_kernel, bands), grid=(clon // block...  19.5 us

profile of v2, /device:TPU:9, one launch (start us, length us, event | category | flops | bytes accessed | tf_op | source)
XLA Modules:
  0.0 443.6 jit_solution(14830474130255952694)
XLA Ops:
  0.0 0.0 copy-start
  0.0 1.1 copy-done
  1.1 0.0 copy-start.1
  1.1 1.1 copy-done.1
  2.2 0.0 copy-start.2
  2.2 1.1 copy-done.2
  3.3 0.0 copy-start.3
  3.4 1.1 copy-done.3
  4.5 0.0 copy-start.4
  4.5 0.7 copy-done.4
  5.1 0.0 copy-start.5
  5.2 0.7 copy-done.5
  5.8 418.3 %filter_exchange.1 = (f32[148,128,128]{2,1,0:T(8,128)}, f32[144,8,128]{2,1,0:T(8,128)S(1)}, f32[144,8,128]{2,1,0:T(8,128)S(1)}, f32[1,128,128]{2,1,0:T(8,128)S(1)}, f32[144,8,128]{2,1,0:T(8,128)S(1)}) custom-call(s32[512]{0:T(512)S(1)} %copy-done.4, s32[512]{0:T(512)S(1)} %copy-done.5, f32[144,128,128]{2,1,0:T(8,128)} %tracer.1, ...), custom_call_target="tpu_custom_call" | custom-call | tf_op jit(solution)/shard_map/filter_exchange/pallas_call | solution.py:217
  424.1 19.5 %flux_step.1 = f32[144,128,128]{2,1,0:T(8,128)} custom-call(f32[148,128,128]{2,1,0:T(8,128)} %get-tuple-element.10.field, f32[2,144,128,128]{3,2,1,0:T(8,128)} %speed_y.1, f32[2,144,128,128]{3,2,1,0:T(8,128)} %speed_y.1, f32[1,128,128]{2,1,0:T(8,128)S(1)} %get-tuple-element.11.edge_x, f32[2,144,128,128]{3,2,1,0:T(8,128)} %speed_y.1, ...), custom_call_target="tpu_custom_call" | custom-call | tf_op jit(solution)/shard_map/flux_step/pallas_call | solution.py:268
Async XLA Ops:
  0.0 1.1 copy-start
  1.1 1.1 copy-start.1
  2.2 1.1 copy-start.2
  3.3 1.1 copy-start.3
  4.5 0.7 copy-start.4
  5.1 0.7 copy-start.5

commit v3 on v2

--- a/solution.py
+++ b/solution.py
@@ -169,12 +169,14 @@
             for j, peer in enumerate(peers)
         ]
         own.start()
-        for copy in sent:
+        for j, copy in enumerate(sent):
+            if c + 1 < chunks:
+                there[c + 1][1][j].wait_send()
+            elif chunks == 1:
+                there[c][1][j].wait_send()
             copy.start()
         back.append((own, sent))
 
-    for copy in there[-1][1]:
-        copy.wait_send()
     go_x.wait()
     for c in range(chunks):
         own, sent = back[c]
@@ -209,7 +211,7 @@
     chunks = clat // devices // 8
     tables = [jnp.asarray(t) for t in hartley_tables(nlon)]
     smem = pl.BlockSpec(memory_space=pltpu.SMEM)
-    hbm = pl.BlockSpec(memory_space=pl.ANY)
+    hbm = pl.BlockSpec(memory_space=pltpu.HBM)
     dma = pltpu.SemaphoreType.DMA
     pairs, alone = dma((chunks, devices - 1)), dma((chunks,))
     shape = lambda *dims: jax.ShapeDtypeStruct(dims, jnp.float32)
@@ -223,7 +225,7 @@
         + [pltpu.VMEM((half, half), jnp.bfloat16)] * 4
         + [dma((4,)), pairs, pairs, alone, pairs, pairs, alone, dma((4,)), dma((4,))],
         compiler_params=pltpu.CompilerParams(
-            collective_id=0, has_side_effects=True, vmem_limit_bytes=48 << 20),
+            collective_id=0, has_side_effects=True, vmem_limit_bytes=65000 << 10),
         name="filter_exchange",
     )(polar_mask, cutoff, tracer, courant, *tables)
 
@@ -233,16 +235,18 @@
     return jnp.minimum(jnp.maximum(face, jnp.minimum(low, high)), jnp.maximum(low, high))
 
 
-def flux_kernel(bands, field, speed_x, next_x, edge_x, speed_y, edge_y, before, after, out, tall, flux):
+def flux_kernel(bands, field, speed_x, next_x, edge_x, speed_y, edge_y, before, after, out, beyond,
+                *scratch):
     count, clat = out.shape[0], out.shape[1]
     final = pl.program_id(0) == pl.num_programs(0) - 1
+    talls, fluxes = scratch[:len(scratch) // 2], scratch[len(scratch) // 2:]
     lat = lax.axis_index("lat")
     top, bottom = lat > 0, lat < bands - 1
 
     def flux_x(i, speed):
         return speed * limited(field[i], field[i + 1], field[i + 2], field[i + 3])
 
-    def column(c, low_flux, speed):
+    def column(c, low_flux, speed, tall, flux):
         high_flux = flux_x(c + 1, speed)
         value = field[c + 2]
         tall[8:8 + clat] = value
@@ -256,14 +260,26 @@
         out[c] = value - (high_flux - low_flux) - (flux[1:clat + 1] - flux[0:clat])
         return high_flux
 
-    carry = flux_x(0, speed_x[0])
-    carry = lax.fori_loop(0, count - 1, lambda c, low: column(c, low, speed_x[c + 1]), carry)
-    column(count - 1, carry, jnp.where(final, edge_x[0], next_x[0]))
+    beyond[...] = jnp.where(final, edge_x[0], next_x[0])
+    group = len(talls)
+    steps = count // group
+
+    def columns(p, carry):
+        for g in range(group):
+            c = p * group + g
+            speed = speed_x[jnp.minimum(c + 1, count - 1)]
+            if g == group - 1:
+                speed = jnp.where(p == steps - 1, beyond[...], speed)
+            carry = column(c, carry, speed, talls[g], fluxes[g])
+        return carry
+
+    lax.fori_loop(0, steps, columns, flux_x(0, speed_x[0]))
 
 
 def advect(field, before, after, edge_x, edge_y, courant, bands):
     _, clon, clat, nf = courant.shape
     block = math.gcd(clon, 16)
+    group = math.gcd(block, 4)
     squeezed = pl.Squeezed()
     return pl.pallas_call(
         functools.partial(flux_kernel, bands),
@@ -282,9 +298,10 @@
             pl.BlockSpec((block, 8, nf), lambda i: (i, 0, 0)),
         ],
         out_specs=pl.BlockSpec((block, clat, nf), lambda i: (i, 0, 0)),
-        scratch_shapes=[pltpu.VMEM((clat + 16, nf), jnp.float32),
-                        pltpu.VMEM((clat + 8, nf), jnp.float32)],
-        compiler_params=pltpu.CompilerParams(vmem_limit_bytes=48 << 20),
+        scratch_shapes=[pltpu.VMEM((clat, nf), jnp.float32)]
+        + [pltpu.VMEM((clat + 16, nf), jnp.float32)] * group
+        + [pltpu.VMEM((clat + 8, nf), jnp.float32)] * group,
+        compiler_params=pltpu.CompilerParams(vmem_limit_bytes=65000 << 10),
         name="flux_step",
     )(field, courant, courant, edge_x, courant, edge_y, before, after)
 

time: 444 us -> 438 us (0.986)
  local copies, waits for them, and re-layouts: 5.82 us -> 0 us
    unnamed x12 -> x0, local copies, waits for them, and re-layouts: 5.82 us -> none
where the time goes in v3:
time: 438 us
  Pallas kernels  438 us (100%)
    pallas_call x1, Pallas kernels, by_kernel(): pl.pallas_call(functools.partial(filter_kernel, devices, bands, chunks),...  417 us
    pallas_call x1, Pallas kernels, advect(): pl.pallas_call(functools.partial(flux_kernel, bands), grid=(clon // block...  20.6 us

profile of v3, /device:TPU:9, one launch (start us, length us, event | category | flops | bytes accessed | tf_op | source)
XLA Modules:
  0.0 437.7 jit_solution(9680192597940030634)
XLA Ops:
  0.0 417.2 %filter_exchange.1 = (f32[148,128,128]{2,1,0:T(8,128)}, f32[144,8,128]{2,1,0:T(8,128)}, f32[144,8,128]{2,1,0:T(8,128)}, f32[1,128,128]{2,1,0:T(8,128)}, f32[144,8,128]{2,1,0:T(8,128)}) custom-call(s32[512]{0:T(512)} %mask_ref.1, s32[512]{0:T(512)} %cut_ref.1, f32[144,128,128]{2,1,0:T(8,128)} %tracer.1, f32[2,144,128,128]{3,2,1,0:T(8,128)} %speed_y.1, ...), custom_call_target="tpu_custom_call" | custom-call | tf_op jit(solution)/shard_map/filter_exchange/pallas_call | solution.py:219
  417.2 20.6 %flux_step.1 = f32[144,128,128]{2,1,0:T(8,128)} custom-call(f32[148,128,128]{2,1,0:T(8,128)} %get-tuple-element.10.field, f32[2,144,128,128]{3,2,1,0:T(8,128)} %speed_y.1, f32[2,144,128,128]{3,2,1,0:T(8,128)} %speed_y.1, f32[1,128,128]{2,1,0:T(8,128)} %get-tuple-element.11.edge_x, f32[2,144,128,128]{3,2,1,0:T(8,128)} %speed_y.1, ...), custom_call_target="tpu_custom_call" | custom-call | tf_op jit(solution)/shard_map/flux_step/pallas_call | solution.py:284

commit v4 on v2

--- a/solution.py
+++ b/solution.py
@@ -94,9 +94,7 @@
             for j, peer in enumerate(peers)
         ]
         own.start()
-        for j, copy in enumerate(sent):
-            if c:
-                there[-1][1][j].wait_send()
+        for copy in sent:
             copy.start()
         there.append((own, sent))
 
@@ -173,8 +171,9 @@
             copy.start()
         back.append((own, sent))
 
-    for copy in there[-1][1]:
-        copy.wait_send()
+    for own, sent in there:
+        for copy in sent:
+            copy.wait_send()
     go_x.wait()
     for c in range(chunks):
         own, sent = back[c]
@@ -209,7 +208,7 @@
     chunks = clat // devices // 8
     tables = [jnp.asarray(t) for t in hartley_tables(nlon)]
     smem = pl.BlockSpec(memory_space=pltpu.SMEM)
-    hbm = pl.BlockSpec(memory_space=pl.ANY)
+    hbm = pl.BlockSpec(memory_space=pltpu.HBM)
     dma = pltpu.SemaphoreType.DMA
     pairs, alone = dma((chunks, devices - 1)), dma((chunks,))
     shape = lambda *dims: jax.ShapeDtypeStruct(dims, jnp.float32)
@@ -223,7 +222,7 @@
         + [pltpu.VMEM((half, half), jnp.bfloat16)] * 4
         + [dma((4,)), pairs, pairs, alone, pairs, pairs, alone, dma((4,)), dma((4,))],
         compiler_params=pltpu.CompilerParams(
-            collective_id=0, has_side_effects=True, vmem_limit_bytes=48 << 20),
+            collective_id=0, has_side_effects=True, vmem_limit_bytes=65000 << 10),
         name="filter_exchange",
     )(polar_mask, cutoff, tracer, courant, *tables)
 
@@ -284,7 +283,7 @@
         out_specs=pl.BlockSpec((block, clat, nf), lambda i: (i, 0, 0)),
         scratch_shapes=[pltpu.VMEM((clat + 16, nf), jnp.float32),
                         pltpu.VMEM((clat + 8, nf), jnp.float32)],
-        compiler_params=pltpu.CompilerParams(vmem_limit_bytes=48 << 20),
+        compiler_params=pltpu.CompilerParams(vmem_limit_bytes=65000 << 10),
         name="flux_step",
     )(field, courant, courant, edge_x, courant, edge_y, before, after)
 

time: 444 us -> 438 us (0.986)
  local copies, waits for them, and re-layouts: 5.82 us -> 0 us
    unnamed x12 -> x0, local copies, waits for them, and re-layouts: 5.82 us -> none
where the time goes in v4:
time: 438 us; the launch traced here: 437 us
  Pallas kernels  437 us (100%)
    pallas_call x1, Pallas kernels, by_kernel(): pl.pallas_call(functools.partial(filter_kernel, devices, bands, chunks),...  417 us
    pallas_call x1, Pallas kernels, advect(): pl.pallas_call(functools.partial(flux_kernel, bands), grid=(clon // block...  20.3 us

profile of v4, /device:TPU:9, one launch (start us, length us, event | category | flops | bytes accessed | tf_op | source)
XLA Modules:
  0.0 437.5 jit_solution(17492814466959497094)
XLA Ops:
  0.0 417.2 %filter_exchange.1 = (f32[148,128,128]{2,1,0:T(8,128)}, f32[144,8,128]{2,1,0:T(8,128)}, f32[144,8,128]{2,1,0:T(8,128)}, f32[1,128,128]{2,1,0:T(8,128)}, f32[144,8,128]{2,1,0:T(8,128)}) custom-call(s32[512]{0:T(512)} %mask_ref.1, s32[512]{0:T(512)} %cut_ref.1, f32[144,128,128]{2,1,0:T(8,128)} %tracer.1, f32[2,144,128,128]{3,2,1,0:T(8,128)} %speed_y.1, ...), custom_call_target="tpu_custom_call" | custom-call | tf_op jit(solution)/shard_map/filter_exchange/pallas_call | solution.py:216
  417.2 20.3 %flux_step.1 = f32[144,128,128]{2,1,0:T(8,128)} custom-call(f32[148,128,128]{2,1,0:T(8,128)} %get-tuple-element.10.field, f32[2,144,128,128]{3,2,1,0:T(8,128)} %speed_y.1, f32[2,144,128,128]{3,2,1,0:T(8,128)} %speed_y.1, f32[1,128,128]{2,1,0:T(8,128)} %get-tuple-element.11.edge_x, f32[2,144,128,128]{3,2,1,0:T(8,128)} %speed_y.1, ...), custom_call_target="tpu_custom_call" | custom-call | tf_op jit(solution)/shard_map/flux_step/pallas_call | solution.py:267
